TPU v7x, 512 devices: a whole 4x8x8 slice. The times are simulated.
512 devices in a mesh: dp: 8 (over z), seq: 64 (over x, y, core).
Axes of the slice: x: 4, y: 8, z: 8, core: 2. Of those that a mesh axis runs over, the one named last changes fastest.
Arguments:
- head_queries: bfloat16 [8, 8192, 3072], P('dp', 'seq')
- head_keys: bfloat16 [8, 8192, 3072], P('dp', 'seq')
- head_values: bfloat16 [8, 8192, 3072], P('dp', 'seq'), may hold values from -6 to 6
- output_gradient: bfloat16 [8, 8192, 3072], P('dp', 'seq'), may hold values from -256 to 256
- key_adapter_input: bfloat16 [8, 8192, 64], P('dp', 'seq'), may hold values from -0.0234375 to 0.0234375
- value_adapter_input: bfloat16 [8, 8192, 64], P('dp', 'seq'), may hold values from -0.0234375 to 0.0234375
- key_block_lists: int32 [24, 64, 5], replicated, may hold values from 0 to 63, as said below
- live_block_counts: int32 [24, 64], replicated, may hold values from 1 to 5, as said below
Outputs:
- key_gradient: bfloat16 [8, 8192, 3072], P('dp', 'seq')
- value_gradient: bfloat16 [8, 8192, 3072], P('dp', 'seq')
- key_adapter_gradient: float32 [3072, 64], P(('dp', 'seq'))
- value_adapter_gradient: float32 [3072, 64], P(('dp', 'seq'))
Inputs may be any that keep to these rules, and one draw needn't show every extreme that they name: Entry 0 of key_block_lists[h, b] is b; the first live_block_counts[h, b] entries are distinct blocks within 2 of b; later entries equal b. live_block_counts[h, b] is the smaller of a count of head h and the number of blocks within 2 of b.
All inputs are finite; a program needn't handle non-finite values.
Results may differ from a plain program's by a relative error of at most 0.04.
Values may be sent and summed in bfloat16 or wider, within the bound.
A program may use at most 64 MiB of HBM per device.

v0:
```python
import jax
import jax.numpy as jnp
from jax import lax
from jax.sharding import PartitionSpec as P

HEAD_COUNT = 24
HEAD_WIDTH = 128
BLK = 128
REACH = 2


def from_partner(block, axis, bit):
    count = lax.axis_size(axis)
    route = []
    for low in range(count):
        high = low | 1 << bit
        if high != low and high < count:
            route += [(low, high), (high, low)]
    return lax.ppermute(block, axis, route)


def passed_along(value, axis, steps):
    count = lax.axis_size(axis)
    leading, last = (max(0, -steps), min(count, count - steps))
    return lax.ppermute(value, axis, [(source, source + steps) for source in range(leading, last)])


def halves(array, bit_dim, bit_value):
    outgoing = lax.dynamic_slice_in_dim(array, 1 - bit_value, 1, axis=bit_dim)
    staying = lax.dynamic_slice_in_dim(array, bit_value, 1, axis=bit_dim)
    return (staying, outgoing)


def rejoin(staying, incoming, bit_dim, bit_value):
    lower_first = jnp.concatenate([staying, incoming], axis=bit_dim)
    upper_first = jnp.concatenate([incoming, staying], axis=bit_dim)
    return jnp.where(bit_value == 0, lower_first, upper_first)


def head_gradients(query_tiles, grad_tiles, key_window, value_window, slots, head_counts):
    scaling = HEAD_WIDTH ** (-0.5)
    query_count = query_tiles.shape[0]
    window_len = key_window.shape[0]
    longest = jnp.max(head_counts)

    def tile_scores(tile_index):
        picked = lax.dynamic_index_in_dim(slots, tile_index, axis=1, keepdims=False)
        key_block = jnp.take(key_window, picked, axis=0)
        scores = (
            jnp.einsum("qxd,qyd->qxy", query_tiles, key_block, preferred_element_type=jnp.float32)
            * scaling
        )
        live = (tile_index < head_counts)[:, None, None]
        return (picked, scores, live)

    def tile_dprobs(picked):
        value_block = jnp.take(value_window, picked, axis=0)
        return jnp.einsum(
            "qxd,qyd->qxy", grad_tiles, value_block, preferred_element_type=jnp.float32
        )

    def stats_pass(tile_index, carry):
        row_max, row_total = carry
        picked, scores, live = tile_scores(tile_index)
        tile_max = jnp.max(jnp.where(live, scores, -jnp.inf), axis=2, keepdims=True)
        new_max = jnp.maximum(row_max, tile_max)
        added = jnp.sum(jnp.where(live, jnp.exp(scores - new_max), 0.0), axis=2, keepdims=True)
        return (new_max, row_total * jnp.exp(row_max - new_max) + added)

    start_max = jnp.full((query_count, BLK, 1), -jnp.inf, jnp.float32)
    start_total = jnp.zeros((query_count, BLK, 1), jnp.float32)
    row_max, row_total = lax.fori_loop(0, longest, stats_pass, (start_max, start_total))

    def probabilities(scores, live):
        return jnp.where(live, jnp.exp(scores - row_max), 0.0) / row_total

    def delta_pass(tile_index, row_delta):
        picked, scores, live = tile_scores(tile_index)
        soft_rounded = probabilities(scores, live).astype(jnp.bfloat16)
        dprobs = tile_dprobs(picked)
        return row_delta + jnp.sum(soft_rounded.astype(jnp.float32) * dprobs, axis=2, keepdims=True)

    row_delta = lax.fori_loop(0, longest, delta_pass, jnp.zeros((query_count, BLK, 1), jnp.float32))

    def gradient_pass(tile_index, buffers):
        key_acc, value_acc = buffers
        picked, scores, live = tile_scores(tile_index)
        soft_probs = probabilities(scores, live)
        soft_rounded = soft_probs.astype(jnp.bfloat16)
        dprobs = tile_dprobs(picked)
        score_grad = (soft_probs * (dprobs - row_delta)).astype(jnp.bfloat16)
        value_add = jnp.einsum(
            "qxy,qxd->qyd", soft_rounded, grad_tiles, preferred_element_type=jnp.float32
        )
        key_add = (
            jnp.einsum("qxy,qxd->qyd", score_grad, query_tiles, preferred_element_type=jnp.float32)
            * scaling
        )
        return (key_acc.at[picked].add(key_add), value_acc.at[picked].add(value_add))

    empty = jnp.zeros((window_len, BLK, HEAD_WIDTH), jnp.float32)
    return lax.fori_loop(0, longest, gradient_pass, (empty, empty))


def body(
    head_queries,
    head_keys,
    head_values,
    output_gradient,
    key_adapter_input,
    value_adapter_input,
    key_block_lists,
    live_block_counts,
):
    team_size = 8
    level_steps = team_size.bit_length() - 1
    heads_local = HEAD_COUNT // team_size
    tokens = head_queries.shape[1]
    position = lax.axis_index("seq")
    member = position % team_size
    team_index = position // team_size
    stacked = jnp.stack(
        [head_queries[0], head_keys[0], head_values[0], output_gradient[0]]
    ).reshape(4, tokens, HEAD_COUNT, HEAD_WIDTH)
    head_order = jnp.arange(HEAD_COUNT, dtype=jnp.int32)
    moving = stacked.reshape((4, tokens) + (2,) * level_steps + (heads_local, HEAD_WIDTH))
    for bit_index in range(level_steps):
        bit_dim = 2 + level_steps - 1 - bit_index
        bit_value = member // (1 << bit_index) % 2
        staying, outgoing = halves(moving, bit_dim, bit_value)
        incoming = from_partner(outgoing, "seq", bit_index)
        moving = rejoin(staying, incoming, bit_dim, bit_value)
    own_blocks = team_size * tokens // BLK
    regrouped = moving.reshape(4, tokens, team_size, heads_local, HEAD_WIDTH).transpose(
        0, 3, 2, 1, 4
    )
    right_edge = regrouped[1:3, :, own_blocks - REACH :]
    left_edge = regrouped[1:3, :, :REACH]
    from_left = passed_along(right_edge, "seq", team_size)
    from_right = passed_along(left_edge, "seq", -team_size)
    key_window = jnp.concatenate([from_left, regrouped[1:3], from_right], axis=2)
    first_query = team_index * own_blocks
    first_key = first_query - REACH
    key_parts = []
    value_parts = []
    for head_slot in range(heads_local):
        head_id = head_order[member * heads_local + head_slot]
        head_lists = lax.dynamic_slice_in_dim(key_block_lists[head_id], first_query, own_blocks, 0)
        head_counts = lax.dynamic_slice_in_dim(
            live_block_counts[head_id], first_query, own_blocks, 0
        )
        slots = head_lists - first_key
        key_acc, value_acc = head_gradients(
            regrouped[0, head_slot],
            regrouped[3, head_slot],
            key_window[0, head_slot],
            key_window[1, head_slot],
            slots,
            head_counts,
        )
        key_parts.append(key_acc)
        value_parts.append(value_acc)
    partials = jnp.stack([jnp.stack(key_parts), jnp.stack(value_parts)])
    lower_partial = partials[:, :, :REACH]
    upper_partial = partials[:, :, own_blocks + REACH :]
    from_lower_team = passed_along(upper_partial.astype(jnp.bfloat16), "seq", team_size).astype(
        upper_partial.dtype
    )
    from_upper_team = passed_along(lower_partial.astype(jnp.bfloat16), "seq", -team_size).astype(
        lower_partial.dtype
    )
    core = partials[:, :, REACH : REACH + own_blocks]
    core = core.at[:, :, :REACH].add(from_lower_team)
    core = core.at[:, :, own_blocks - REACH :].add(from_upper_team)
    gradients = core.astype(jnp.bfloat16)
    homeward = gradients.transpose(0, 3, 2, 1, 4)
    going_home = homeward.reshape((2, tokens) + (2,) * level_steps + (heads_local, HEAD_WIDTH))
    for bit_index in range(level_steps):
        bit_dim = 2 + level_steps - 1 - bit_index
        bit_value = member // (1 << bit_index) % 2
        staying, outgoing = halves(going_home, bit_dim, bit_value)
        incoming = from_partner(outgoing, "seq", bit_index)
        going_home = rejoin(staying, incoming, bit_dim, bit_value)
    received_block = going_home.reshape(2, tokens, HEAD_COUNT, HEAD_WIDTH)
    received_block = received_block.reshape(2, tokens, HEAD_COUNT * HEAD_WIDTH)
    contract_dims = (((0,), (0,)), ((), ()))
    key_adapter_term = lax.dot_general(
        received_block[0], key_adapter_input[0], contract_dims, preferred_element_type=jnp.float32
    )
    value_adapter_term = lax.dot_general(
        received_block[1], value_adapter_input[0], contract_dims, preferred_element_type=jnp.float32
    )
    key_adapter_gradient, value_adapter_gradient = (
        lax.psum_scatter(key_adapter_term, ("dp", "seq"), scatter_dimension=0, tiled=True),
        lax.psum_scatter(value_adapter_term, ("dp", "seq"), scatter_dimension=0, tiled=True),
    )
    return (
        received_block[0][None],
        received_block[1][None],
        key_adapter_gradient,
        value_adapter_gradient,
    )


def solution(mesh):
    in_specs = (
        P("dp", "seq", None),
        P("dp", "seq", None),
        P("dp", "seq", None),
        P("dp", "seq", None),
        P("dp", "seq", None),
        P("dp", "seq", None),
        P(),
        P(),
    )
    out_specs = (
        P("dp", "seq", None),
        P("dp", "seq", None),
        P(("dp", "seq"), None),
        P(("dp", "seq"), None),
    )
    return jax.shard_map(body, mesh=mesh, in_specs=in_specs, out_specs=out_specs, check_vma=False)
```

profile of v0, /device:TPU:1, one launch (start us, length us, event | category | flops | bytes accessed | tf_op | source)
XLA Modules:
  0.0 839.4 jit_solution(11162836905713291646)
XLA Ops:
  11.8 2.3 copy.64
  17.0 8.7 %collective-permute-start = (bf16[4,128,2,2,1,3,128]{1,6,5,4,3,2,0:T(8,128)(2,1)}, bf16[4,128,2,2,1,3,128]{1,6,5,4,3,2,0:T(8,128)(2,1)}, u32[]{:S(2)}, u32[]{:S(2)}) collective-permute-start(bf16[4,128,2,2,1,3,128]{1,6,5,4,3,2,0:T(8,128)(2,1)} %get-tuple-element.1096), channel_id=1, source_target_pairs={{0,1},{1,0},{2,3},{3,2},{4,5},{5,4},{6,7},{7,6},{8,9},{9,8},{10,11... | collective-permute-start | bytes 4718600 | tf_op jit(solution)/shard_map/ppermute | solution.py:19
  25.8 3.3 collective-permute-done
  29.1 2.1 maximum_select_fusion
  34.7 35.8 %collective-permute-done.1 = bf16[4,128,2,1,2,3,128]{1,6,5,4,3,2,0:T(8,128)(2,1)} collective-permute-done((bf16[4,128,2,1,2,3,128]{1,6,5,4,3,2,0:T(8,128)(2,1)}, bf16[4,128,2,1,2,3,128]{1,6,5,4,3,2,0:T(8,128)(2,1)}, u32[]{:S(2)}, u32[]{:S(2)}) %collective-permute-start.1) | collective-permute-done | bytes 1572896 | tf_op jit(solution)/shard_map/ppermute | solution.py:19
  70.5 2.2 maximum_select_fusion.1
  77.3 69.9 %collective-permute-done.2 = bf16[4,128,1,2,2,3,128]{1,6,5,4,3,2,0:T(8,128)(2,1)} collective-permute-done((bf16[4,128,1,2,2,3,128]{1,6,5,4,3,2,0:T(8,128)(2,1)}, bf16[4,128,1,2,2,3,128]{1,6,5,4,3,2,0:T(8,128)(2,1)}, u32[]{:S(2)}, u32[]{:S(2)}) %collective-permute-start.2) | collective-permute-done | bytes 1572896 | tf_op jit(solution)/shard_map/ppermute | solution.py:19
  147.2 3.7 maximum_select_fusion.2
  150.9 4.6 copy.65
  155.6 2.1 fusion.133
  163.0 2.1 dynamic-slice_bitcast_fusion.2
  166.7 2.3 slice_bitcast_fusion.10
  169.0 7.3 collective-permute-done.3
  176.3 8.5 %collective-permute-done.4 = bf16[2,3,2,128,128]{4,3,2,1,0:T(8,128)(2,1)S(1)} collective-permute-done((bf16[2,3,2,128,128]{4,3,2,1,0:T(8,128)(2,1)}, bf16[2,3,2,128,128]{4,3,2,1,0:T(8,128)(2,1)S(1)}, u32[]{:S(2)}, u32[]{:S(2)}) %collective-permute-start.4) | collective-permute-done | bytes 393248 | tf_op jit(solution)/shard_map/ppermute | solution.py:25
  186.7 10.0 %while.104 = (s32[]{:T(128)}, f32[8,128,1]{1,0,2:T(8,128)}, f32[8,128,1]{1,0,2:T(8,128)S(1)}, s32[]{:T(128)}, s32[8]{0:T(128)S(1)}, /*index=5*/s32[8,5]{0,1:T(8,...) while((s32[]{:T(128)}, f32[8,128,1]{1,0,2:T(8,128)}, ...), condition=%wide.region_4.6_spmd, body=%wide.region_1.5_spmd.sunk | while | flops 34475068 | bytes 2154847 | solution.py:72
  197.3 12.3 %while.105 = (s32[]{:T(128)}, f32[8,128,1]{1,2,0:T(1,128)}, s32[]{:T(128)}, s32[8]{0:T(128)S(1)}, s32[8,5]{0,1:T(8,128)S(1)}, /*index=5*/bf16[12,128,128]{2,1,0:...) while((s32[]{:T(128)}, f32[8,128,1]{1,2,0:T(1,128)}, ...), condition=%wide.region_7.9_spmd, body=%wide.region_5.8_spmd.sunk | while | flops 68420672 | bytes 3174807 | solution.py:83
  211.5 26.0 %while.106 = (s32[]{:T(128)}, f32[12,128,128]{2,1,0:T(8,128)}, f32[12,128,128]{2,1,0:T(8,128)}, s32[]{:T(128)}, s32[8,5]{0,1:T(8,128)S(1)}, /*index=5*/s32[8]{0:...) while((s32[]{:T(128)}, f32[12,128,128]{2,1,0:T(8,128)}, ...), condition=%wide.region_11.13_spmd, body=%wide.region_8.12_spmd.sunk | while | flops 135922768 | bytes 8440235 | solution.py:102
  218.5 2.7 scatter_fusion
  221.4 2.8 scatter_fusion.1
  231.2 2.6 scatter_fusion
  234.1 2.8 scatter_fusion.1
  238.1 30.6 %while.107 = (s32[]{:T(128)}, f32[8,128,1]{1,0,2:T(8,128)}, f32[8,128,1]{1,0,2:T(8,128)}, s32[]{:T(128)}, s32[8]{0:T(128)}, /*index=5*/s32[8,5]{0,1:T(8,128)}, b...) while((s32[]{:T(128)}, f32[8,128,1]{1,0,2:T(8,128)}, ...), condition=%wide.region_16.18_spmd, body=%wide.region_13.17_spmd.sunk | while | flops 34475068 | bytes 2154847 | solution.py:72
  269.3 28.4 %while.108 = (s32[]{:T(128)}, f32[8,128,1]{1,2,0:T(1,128)}, s32[]{:T(128)}, s32[8]{0:T(128)}, s32[8,5]{0,1:T(8,128)}, /*index=5*/bf16[12,128,128]{2,1,0:T(8,128)...) while((s32[]{:T(128)}, f32[8,128,1]{1,2,0:T(1,128)}, ...), condition=%wide.region_19.21_spmd, body=%wide.region_17.20_spmd.sunk | while | flops 68420672 | bytes 3174807 | solution.py:83
  299.6 57.5 %while.109 = (s32[]{:T(128)}, f32[12,128,128]{2,1,0:T(8,128)}, f32[12,128,128]{2,1,0:T(8,128)}, s32[]{:T(128)}, s32[8,5]{0,1:T(8,128)}, /*index=5*/s32[8]{0:T(12...) while((s32[]{:T(128)}, f32[12,128,128]{2,1,0:T(8,128)}, ...), condition=%wide.region_23.25_spmd, body=%wide.region_20.24_spmd.sunk | while | flops 135922768 | bytes 9454211 | solution.py:102
  305.4 2.7 scatter_fusion.2
  308.3 2.7 scatter_fusion.3
  316.8 2.7 scatter_fusion.2
  319.7 2.7 scatter_fusion.3
  328.2 2.7 scatter_fusion.2
  331.1 2.7 scatter_fusion.3
  339.6 2.7 scatter_fusion.2
  342.4 2.7 scatter_fusion.3
  350.9 2.6 scatter_fusion.2
  353.8 2.6 scatter_fusion.3
  357.0 8.2 while.110
  365.3 8.8 %while.111 = (s32[]{:T(128)}, f32[8,128,1]{1,2,0:T(1,128)S(1)}, s32[]{:T(128)}, s32[8]{0:T(128)}, s32[8,5]{0,1:T(8,128)}, /*index=5*/bf16[12,128,128]{2,1,0:T(8,...) while((s32[]{:T(128)}, f32[8,128,1]{1,2,0:T(1,128)S(1)}, ...), condition=%wide.region_31.33_spmd, body=%wide.region_29.32_spmd.sunk | while | flops 68420672 | bytes 3174807 | solution.py:83
  375.1 18.1 %while.112 = (s32[]{:T(128)}, f32[12,128,128]{2,1,0:T(8,128)S(1)}, f32[12,128,128]{2,1,0:T(8,128)}, s32[]{:T(128)}, s32[8,5]{0,1:T(8,128)}, /*index=5*/s32[8]{0:...) while((s32[]{:T(128)}, f32[12,128,128]{2,1,0:T(8,128)S(1)}, ...), condition=%wide.region_35.37_spmd, body=%wide.region_32.36_spmd.sunk | while | flops 135922768 | bytes 8405547 | solution.py:102
  381.2 2.7 scatter_fusion.5
  389.9 2.6 scatter_fusion.5
  395.9 14.5 %collective-permute-start.5 = (bf16[2,3,2,128,128]{4,3,2,1,0:T(8,128)(2,1)S(1)}, bf16[2,3,2,128,128]{4,3,2,1,0:T(8,128)(2,1)S(1)}, u32[]{:S(2)}, u32[]{:S(2)}) collective-permute-start(bf16[2,3,2,128,128]{4,3,2,1,0:T(8,128)(2,1)S(1)} %get-tuple-element.1098), channel_id=1, source_target_pairs={{0,8},{1,9},{2,10},{3,11},{4,12},{5,13},{6,14},{7,15},{8,16},{9,17... | collective-permute-start | bytes 1179656 | tf_op jit(solution)/shard_map/ppermute | solution.py:25
  411.9 6.1 collective-permute-done.5
  418.0 8.0 collective-permute-done.6
  431.6 2.3 collective-permute-done.7
  434.2 21.4 %collective-permute-start.8 = (bf16[2,128,2,1,2,3,128]{1,6,5,4,3,2,0:T(8,128)(2,1)S(1)}, bf16[2,128,2,1,2,3,128]{1,6,5,4,3,2,0:T(8,128)(2,1)S(1)}, u32[]{:S(2)}, u32[]{:S(2)}) collective-permute-start(bf16[2,128,2,1,2,3,128]{1,6,5,4,3,2,0:T(8,128)(2,1)S(1)} %get-tuple-element.1110), channel_id=1, source_target_pairs={{0,2},{2,0},{1,3},{3,1},{4,6},{6,4},{5,7},{7,5},{8,10},{10,8},{9,1... | collective-permute-start | bytes 2359304 | tf_op jit(solution)/shard_map/ppermute | solution.py:19
  455.6 21.7 %collective-permute-done.8 = bf16[2,128,2,1,2,3,128]{1,6,5,4,3,2,0:T(8,128)(2,1)S(1)} collective-permute-done((bf16[2,128,2,1,2,3,128]{1,6,5,4,3,2,0:T(8,128)(2,1)S(1)}, bf16[2,128,2,1,2,3,128]{1,6,5,4,3,2,0:T(8,128)(2,1)S(1)}, u32[]{:S(2)}, u32[]{:S(2)}) %collective-permute-start.8) | collective-permute-done | bytes 786464 | tf_op jit(solution)/shard_map/ppermute | solution.py:19
  477.7 28.7 %collective-permute-start.9 = (bf16[2,128,1,2,2,3,128]{1,6,5,4,3,2,0:T(8,128)(2,1)S(1)}, bf16[2,128,1,2,2,3,128]{1,6,5,4,3,2,0:T(8,128)(2,1)S(1)}, u32[]{:S(2)}, u32[]{:S(2)}) collective-permute-start(bf16[2,128,1,2,2,3,128]{1,6,5,4,3,2,0:T(8,128)(2,1)S(1)} %get-tuple-element.1108), channel_id=1, source_target_pairs={{0,4},{4,0},{1,5},{5,1},{2,6},{6,2},{3,7},{7,3},{8,12},{12,8},{9,1... | collective-permute-start | bytes 2359304 | tf_op jit(solution)/shard_map/ppermute | solution.py:19
  506.3 34.0 %collective-permute-done.9 = bf16[2,128,1,2,2,3,128]{1,6,5,4,3,2,0:T(8,128)(2,1)S(1)} collective-permute-done((bf16[2,128,1,2,2,3,128]{1,6,5,4,3,2,0:T(8,128)(2,1)S(1)}, bf16[2,128,1,2,2,3,128]{1,6,5,4,3,2,0:T(8,128)(2,1)S(1)}, u32[]{:S(2)}, u32[]{:S(2)}) %collective-permute-start.9) | collective-permute-done | bytes 786464 | tf_op jit(solution)/shard_map/ppermute | solution.py:19
  546.2 283.8 %all-reduce.5.cloned.1.call-done = (f32[3072,64]{1,0:T(8,128)}, f32[3072,64]{1,0:T(8,128)}) async-done(((f32[3072,64]{1,0:T(8,128)}, f32[3072,64]{1,0:T(8,128)}), (f32[3072,64]{1,0:T(8,128)}, f32[3072,64]{1,0:T(8,128)})) %all-reduce.5.cloned.1.call-update) | async-done | bytes 1572880
  (339 shorter events, 181.7 us)
Async XLA Ops:
  7.2 533.6 %copy-start = (bf16[1,128,64]{1,2,0:T(8,128)(2,1)S(1)}, bf16[1,128,64]{1,2,0:T(8,128)(2,1)}, u32[]{:S(2)}) copy-start(bf16[1,128,64]{1,2,0:T(8,128)(2,1)} %param.37) | copy-start | bytes 49156
  7.2 822.8 %all-reduce.5.cloned.1.call-start = ((), (), s32[]{:S(2)}) async-start(), calls=%async_computation | async-start | bytes 6291456
  17.0 12.1 %collective-permute-start = (bf16[4,128,2,2,1,3,128]{1,6,5,4,3,2,0:T(8,128)(2,1)}, bf16[4,128,2,2,1,3,128]{1,6,5,4,3,2,0:T(8,128)(2,1)}, u32[]{:S(2)}, u32[]{:S(2)}) collective-permute-start(bf16[4,128,2,2,1,3,128]{1,6,5,4,3,2,0:T(8,128)(2,1)} %get-tuple-element.1096), channel_id=1, source_target_pairs={{0,1},{1,0},{2,3},{3,2},{4,5},{5,4},{6,7},{7,6},{8,9},{9,8},{10,11... | collective-permute-start | bytes 4718600 | tf_op jit(solution)/shard_map/ppermute | solution.py:19
  32.7 37.8 %collective-permute-start.1 = (bf16[4,128,2,1,2,3,128]{1,6,5,4,3,2,0:T(8,128)(2,1)}, bf16[4,128,2,1,2,3,128]{1,6,5,4,3,2,0:T(8,128)(2,1)}, u32[]{:S(2)}, u32[]{:S(2)}) collective-permute-start(bf16[4,128,2,1,2,3,128]{1,6,5,4,3,2,0:T(8,128)(2,1)} %get-tuple-element.1094), channel_id=1, source_target_pairs={{0,2},{2,0},{1,3},{3,1},{4,6},{6,4},{5,7},{7,5},{8,10},{10,8},{9,1... | collective-permute-start | bytes 4718600 | tf_op jit(solution)/shard_map/ppermute | solution.py:19
  74.1 73.1 %collective-permute-start.2 = (bf16[4,128,1,2,2,3,128]{1,6,5,4,3,2,0:T(8,128)(2,1)}, bf16[4,128,1,2,2,3,128]{1,6,5,4,3,2,0:T(8,128)(2,1)}, u32[]{:S(2)}, u32[]{:S(2)}) collective-permute-start(bf16[4,128,1,2,2,3,128]{1,6,5,4,3,2,0:T(8,128)(2,1)} %get-tuple-element.1092), channel_id=1, source_target_pairs={{0,4},{4,0},{1,5},{5,1},{2,6},{6,2},{3,7},{7,3},{8,12},{12,8},{9,1... | collective-permute-start | bytes 4718600 | tf_op jit(solution)/shard_map/ppermute | solution.py:19
  157.6 18.6 %collective-permute-start.3 = (bf16[2,3,2,128,128]{4,3,2,1,0:T(8,128)(2,1)}, bf16[2,3,2,128,128]{4,3,2,1,0:T(8,128)(2,1)S(1)}, u32[]{:S(2)}, u32[]{:S(2)}) collective-permute-start(bf16[2,3,2,128,128]{4,3,2,1,0:T(8,128)(2,1)} %get-tuple-element.1089), channel_id=1, source_target_pairs={{0,8},{1,9},{2,10},{3,11},{4,12},{5,13},{6,14},{7,15},{8,16},{9,17... | collective-permute-start | bytes 1179656 | tf_op jit(solution)/shard_map/ppermute | solution.py:25
  159.7 25.1 %collective-permute-start.4 = (bf16[2,3,2,128,128]{4,3,2,1,0:T(8,128)(2,1)}, bf16[2,3,2,128,128]{4,3,2,1,0:T(8,128)(2,1)S(1)}, u32[]{:S(2)}, u32[]{:S(2)}) collective-permute-start(bf16[2,3,2,128,128]{4,3,2,1,0:T(8,128)(2,1)} %get-tuple-element.1090), channel_id=1, source_target_pairs={{8,0},{9,1},{10,2},{11,3},{12,4},{13,5},{14,6},{15,7},{16,8},{17,9... | collective-permute-start | bytes 1179656 | tf_op jit(solution)/shard_map/ppermute | solution.py:25
  161.0 4.2 copy-start.6
  212.1 3.6 copy-start.7
  212.1 3.6 copy-start.9
  212.2 3.6 copy-start.14
  212.2 3.6 copy-start.12
  217.9 0.6 copy-start.11
  221.2 3.0 copy-start.8
  221.2 3.0 copy-start.10
  221.2 3.0 copy-start.15
  224.9 3.6 copy-start.7
  224.9 3.6 copy-start.9
  224.9 3.6 copy-start.14
  224.9 3.6 copy-start.12
  230.6 0.6 copy-start.11
  233.8 3.0 copy-start.8
  233.8 3.0 copy-start.10
  233.8 3.0 copy-start.15
  238.1 31.2 %copy-start.2 = (bf16[12,128,128]{2,1,0:T(8,128)(2,1)S(1)}, bf16[12,128,128]{2,1,0:T(8,128)(2,1)}, u32[]{:S(2)}) copy-start(bf16[12,128,128]{2,1,0:T(8,128)(2,1)} %get-tuple-element.1992) | copy-start | bytes 1179652
  300.2 3.3 copy-start.5
  301.0 2.6 copy-start.13
  311.6 3.3 copy-start.5
  312.4 2.6 copy-start.13
  323.0 3.3 copy-start.5
  323.8 2.6 copy-start.13
  334.4 3.3 copy-start.5
  335.1 2.6 copy-start.13
  345.7 3.3 copy-start.5
  346.5 2.6 copy-start.13
  357.0 8.2 copy-start.1
  393.2 2.0 copy-start.3
  393.2 2.1 copy-start.4
  395.9 22.0 %collective-permute-start.5 = (bf16[2,3,2,128,128]{4,3,2,1,0:T(8,128)(2,1)S(1)}, bf16[2,3,2,128,128]{4,3,2,1,0:T(8,128)(2,1)S(1)}, u32[]{:S(2)}, u32[]{:S(2)}) collective-permute-start(bf16[2,3,2,128,128]{4,3,2,1,0:T(8,128)(2,1)S(1)} %get-tuple-element.1098), channel_id=1, source_target_pairs={{0,8},{1,9},{2,10},{3,11},{4,12},{5,13},{6,14},{7,15},{8,16},{9,17... | collective-permute-start | bytes 1179656 | tf_op jit(solution)/shard_map/ppermute | solution.py:25
  410.4 15.7 %collective-permute-start.6 = (bf16[2,3,2,128,128]{4,3,2,1,0:T(8,128)(2,1)S(1)}, bf16[2,3,2,128,128]{4,3,2,1,0:T(8,128)(2,1)S(1)}, u32[]{:S(2)}, u32[]{:S(2)}) collective-permute-start(bf16[2,3,2,128,128]{4,3,2,1,0:T(8,128)(2,1)S(1)} %get-tuple-element.1097), channel_id=1, source_target_pairs={{8,0},{9,1},{10,2},{11,3},{12,4},{13,5},{14,6},{15,7},{16,8},{17,9... | collective-permute-start | bytes 1179656 | tf_op jit(solution)/shard_map/ppermute | solution.py:25
  429.7 4.2 collective-permute-start.7
  434.2 43.1 %collective-permute-start.8 = (bf16[2,128,2,1,2,3,128]{1,6,5,4,3,2,0:T(8,128)(2,1)S(1)}, bf16[2,128,2,1,2,3,128]{1,6,5,4,3,2,0:T(8,128)(2,1)S(1)}, u32[]{:S(2)}, u32[]{:S(2)}) collective-permute-start(bf16[2,128,2,1,2,3,128]{1,6,5,4,3,2,0:T(8,128)(2,1)S(1)} %get-tuple-element.1110), channel_id=1, source_target_pairs={{0,2},{2,0},{1,3},{3,1},{4,6},{6,4},{5,7},{7,5},{8,10},{10,8},{9,1... | collective-permute-start | bytes 2359304 | tf_op jit(solution)/shard_map/ppermute | solution.py:19
  477.7 62.7 %collective-permute-start.9 = (bf16[2,128,1,2,2,3,128]{1,6,5,4,3,2,0:T(8,128)(2,1)S(1)}, bf16[2,128,1,2,2,3,128]{1,6,5,4,3,2,0:T(8,128)(2,1)S(1)}, u32[]{:S(2)}, u32[]{:S(2)}) collective-permute-start(bf16[2,128,1,2,2,3,128]{1,6,5,4,3,2,0:T(8,128)(2,1)S(1)} %get-tuple-element.1108), channel_id=1, source_target_pairs={{0,4},{4,0},{1,5},{5,1},{2,6},{6,2},{3,7},{7,3},{8,12},{12,8},{9,1... | collective-permute-start | bytes 2359304 | tf_op jit(solution)/shard_map/ppermute | solution.py:19
  540.6 1.7 copy-start.16
Sparse Core Ops, SparseCore 0:
  543.9 285.9 all-reduce.4
where the time goes:
time: 845 us; the launch traced here: 839 us
  waiting for transfers between devices  481 us (57%)
  other arithmetic  108 us (13%)
  starting transfers between devices  83.6 us (10%)
  local copies, waits for them, and re-layouts  77 us (9%)
  matrix products  50.3 us (6%)
  loops' own time  24.6 us (3%)
  between operations  14.7 us (2%)
    unnamed x2, waiting for transfers between devices  284 us
    ppermute x6, waiting for transfers between devices, from_partner(): return lax.ppermute(block, axis, route)  167 us
    ppermute x6, starting transfers between devices, from_partner(): return lax.ppermute(block, axis, route)  64.5 us
    dot_general x27, matrix products, tile_scores(): jnp.einsum('qxd,qyd->qxy', query_tiles, key_block, preferred_element_type...  32.5 us
    ppermute x4, waiting for transfers between devices, passed_along(): lax.ppermute(value, axis, [(source, source + steps) for source in range(l...  29.9 us
    scatter-add x9, other arithmetic, gradient_pass(): value_acc.at[picked].add(value_add)  24.3 us
    scatter-add x9, other arithmetic, gradient_pass(): key_acc.at[picked].add(key_add)  20.7 us
    ppermute x4, starting transfers between devices, passed_along(): lax.ppermute(value, axis, [(source, source + steps) for source in range(l...  19.1 us
  transfers between devices with their start and end apart: 11, of which 11 were waited for; matrix products, arithmetic and copies ran while one was open for 1% of the time, Pallas kernels for 0%

commit v1 on v0

v1 whole, which is shorter than its diff:
```python
import functools

import jax
import jax.numpy as jnp
from jax import lax
from jax.experimental import pallas as pl
from jax.experimental.pallas import tpu as pltpu
from jax.sharding import PartitionSpec as P

HEAD_WIDTH = 128
BLK = 128
REACH = 2
WINDOW = 2 * REACH + 1
ROW_GROUP = 16
HUGE = 3.0e38
MESH = pl.DeviceIdType.MESH
F32 = jnp.float32
BF16 = jnp.bfloat16
NT = (((1,), (1,)), ((), ()))
NN = (((1,), (0,)), ((), ()))
TN = (((0,), (0,)), ((), ()))
OTHERS = (0, 1, 3, 4)


def kernel(
    planes, ring, heads, group,
    q, k, v, g, ka, va, bias,
    dk, dv, ad,
    hq, hg, es, ds, st, rs, fo, fr, zs, zr, own, xr, rows, ub, yr,
    h_send, h_recv, s_send, s_recv, f_send, f_recv, z_send, z_recv, x_send, x_recv, y_send, y_recv,
):
    scaling = HEAD_WIDTH ** (-0.5)
    z = lax.axis_index("dp")
    pos = lax.axis_index("seq")
    parity = lax.rem(pos, 2)
    partner = pos + 1 - 2 * parity
    width = heads * HEAD_WIDTH
    x_count = ring // group
    x_at = pos // group
    y_at = lax.rem(pos, group)
    x_rows = width // x_count
    y_rows = x_rows // group

    def peer(step):
        return lax.rem(pos + step + ring, ring)

    def x_peer(step):
        return lax.rem(x_at + step, x_count) * group + y_at

    def y_peer(step):
        return x_at * group + lax.rem(y_at + step, group)

    def z_peer(step):
        return lax.rem(z + step, planes)

    def piece(step):
        return lax.rem(z + 1 + step, planes)

    def remote(src, dst, send, recv, device):
        return pltpu.make_async_remote_copy(
            src_ref=src, dst_ref=dst, send_sem=send, recv_sem=recv,
            device_id=device, device_id_type=MESH,
        )

    def halo(flow, i, a, landing=False):
        source, store = (q, g)[a], (hq, hg)[a]
        cols = pl.ds(pl.multiple_of(piece(i) * width, 128), width)
        if flow == 0:
            src, slot, to = source.at[:, cols], 0, peer(2)
        elif flow == 1:
            src, slot, to = source.at[:, cols], 4, peer(-2)
        elif flow == 2:
            src, to = source.at[:, cols], partner
            slot = 3 - 2 * parity if landing else 1 + 2 * parity
        else:
            src, to = store.at[i, 4 - 4 * parity], partner
            slot = 1 + 2 * parity if landing else 3 - 2 * parity
        return remote(
            src, store.at[i, slot], h_send.at[flow, i, a], h_recv.at[flow, i, a], (z, to)
        )

    def stat_copy(j, i):
        return remote(st.at[j, i], rs.at[j, i], s_send.at[j, i], s_recv.at[j, i], (z, peer(j - 2)))

    def final_copy(j, i):
        return remote(fo.at[j, i], fr.at[j, i], f_send.at[j, i], f_recv.at[j, i], (z, peer(2 - j)))

    def z_copy(i):
        return remote(zs.at[i], zr.at[i], z_send.at[i], z_recv.at[i], (piece(i), pos))

    def x_copy(d):
        there = lax.rem(x_at + d, x_count)
        src = own.at[pl.ds(pl.multiple_of(there * x_rows, 8), x_rows)]
        return remote(src, xr.at[d - 1], x_send.at[d - 1], x_recv.at[d - 1], (z, x_peer(d)))

    def y_copy(d):
        there = lax.rem(y_at + d, group)
        return remote(
            ub.at[there], yr.at[d - 1], y_send.at[d - 1], y_recv.at[d - 1], (z, y_peer(d))
        )

    barrier = pltpu.get_barrier_semaphore()
    greeted = 0
    for d in (-2, -1, 1, 2):
        pl.semaphore_signal(barrier, inc=1, device_id=(z, peer(d)), device_id_type=MESH)
        greeted += 1
    for d in range(1, planes):
        pl.semaphore_signal(barrier, inc=1, device_id=(z_peer(d), pos), device_id_type=MESH)
        greeted += 1
    for d in range(1, x_count):
        pl.semaphore_signal(barrier, inc=1, device_id=(z, x_peer(d)), device_id_type=MESH)
        greeted += 1
    for d in range(1, group):
        pl.semaphore_signal(barrier, inc=1, device_id=(z, y_peer(d)), device_id_type=MESH)
        greeted += 1
    pl.semaphore_wait(barrier, greeted)

    @pl.loop(0, planes)
    def _(i):
        for flow in (0, 1, 2):
            for a in (0, 1):
                halo(flow, i, a).start()

    def head_cols(i, h):
        return pl.ds(pl.multiple_of(piece(i) * width + h * HEAD_WIDTH, 128), HEAD_WIDTH)

    def operand(own_ref, store, i, h, j):
        if isinstance(j, int) and j == 2:
            return own_ref[:, head_cols(i, h)]
        return store[i, j, :, h * HEAD_WIDTH : (h + 1) * HEAD_WIDTH]

    def tile_stats(i, h, j):
        held = lax.rem(i, 3)
        scores = scaling * lax.dot_general(
            k[:, head_cols(i, h)], operand(q, hq, i, h, j), NT, preferred_element_type=F32
        )
        dprobs = lax.dot_general(
            v[:, head_cols(i, h)], operand(g, hg, i, h, j), NT, preferred_element_type=F32
        )
        top = jnp.max(scores, axis=0, keepdims=True)
        grown = jnp.exp(scores - top)
        es[held, h, j] = grown
        ds[held, h, j] = dprobs
        st[j, i, 0, h : h + 1, :] = top
        st[j, i, 1, h : h + 1, :] = jnp.sum(grown, axis=0, keepdims=True)
        st[j, i, 2, h : h + 1, :] = jnp.sum(grown * dprobs, axis=0, keepdims=True)

    def first_pass(i):
        for flow in (0, 1):
            for a in (0, 1):
                halo(flow, i, a, True).wait_recv()
        for a in (0, 1):
            halo(3, i, a).start()
        for a in (0, 1):
            halo(2, i, a, True).wait_recv()
        for h in range(heads):
            for j in (2, 0, 4, 3 - 2 * parity):
                tile_stats(i, h, j)
        for a in (0, 1):
            halo(3, i, a, True).wait_recv()
        for h in range(heads):
            tile_stats(i, h, 1 + 2 * parity)
        for j in OTHERS:
            stat_copy(j, i).start()

    def combine(i):
        for j in OTHERS:
            stat_copy(j, i).wait_recv()
        tops, totals, sums, shut = [], [], [], []
        for j in range(WINDOW):
            part = st if j == 2 else rs
            closed = bias[j, piece(i)]
            shut.append(closed)
            tops.append(part[j, i, 0, 0:heads, :] + closed)
            totals.append(part[j, i, 1, 0:heads, :])
            sums.append(part[j, i, 2, 0:heads, :])
        top = functools.reduce(jnp.maximum, tops)
        weights = [jnp.exp(t - top) for t in tops]
        total = sum(w * t for w, t in zip(weights, totals))
        delta = sum(w * t for w, t in zip(weights, sums)) / total
        level = top + jnp.log(total)
        for j in range(WINDOW):
            fo[j, i, 0, 0:heads, :] = jnp.where(shut[j] < 0, HUGE, level)
            fo[j, i, 1, 0:heads, :] = delta
        for j in OTHERS:
            final_copy(j, i).start()

    def second_pass(i):
        held = lax.rem(i, 3)
        for j in OTHERS:
            final_copy(j, i).wait_recv()
        for h in range(heads):
            key_sum = jnp.zeros((BLK, HEAD_WIDTH), F32)
            value_sum = jnp.zeros((BLK, HEAD_WIDTH), F32)
            for j in range(WINDOW):
                final = fo if j == 2 else fr
                factor = jnp.exp(st[j, i, 0, h : h + 1, :] - final[j, i, 0, h : h + 1, :])
                probs = es[held, h, j] * factor
                score_grad = (probs * (ds[held, h, j] - final[j, i, 1, h : h + 1, :])).astype(BF16)
                value_sum += lax.dot_general(
                    probs.astype(BF16), operand(g, hg, i, h, j), NN, preferred_element_type=F32
                )
                key_sum += lax.dot_general(
                    score_grad, operand(q, hq, i, h, j), NN, preferred_element_type=F32
                )
            key_out = (key_sum * scaling).astype(BF16)
            value_out = value_sum.astype(BF16)
            dk[:, head_cols(i, h)] = key_out
            dv[:, head_cols(i, h)] = value_out
            term = lax.dot_general(key_out, ka[...], TN, preferred_element_type=F32)
            term += lax.dot_general(value_out, va[...], TN, preferred_element_type=F32)
            own[h * HEAD_WIDTH : (h + 1) * HEAD_WIDTH, :] = term

        @pl.when(i < planes - 1)
        def _():
            zs[i] = own[...].astype(BF16)
            z_copy(i).start()

    @pl.loop(0, planes + 2)
    def _(t):
        @pl.when(t < planes)
        def _():
            first_pass(t)

        @pl.when((t >= 1) & (t < planes + 1))
        def _():
            combine(t - 1)

        @pl.when(t >= 2)
        def _():
            second_pass(t - 2)

    total = own[...]
    for i in range(planes - 1):
        z_copy(i).wait_recv()
        total += zr[i].astype(F32)
    own[...] = total
    for d in range(1, x_count):
        x_copy(d).start()
    mine = own[pl.ds(pl.multiple_of(x_at * x_rows, 8), x_rows), :]
    for d in range(1, x_count):
        x_copy(d).wait_recv()
        mine += xr[d - 1]
    rows[...] = mine
    ub[...] = jnp.zeros_like(ub)
    for n in range(group):
        ub[n, 0:y_rows, :] = rows[n * y_rows : (n + 1) * y_rows, :]
    for d in range(1, group):
        y_copy(d).start()
    last = ub[y_at]
    for d in range(1, group):
        y_copy(d).wait_recv()
        last += yr[d - 1]
    ad[...] = last

    @pl.loop(0, planes)
    def _(i):
        for flow in range(4):
            for a in (0, 1):
                halo(flow, i, a).wait_send()
        for j in OTHERS:
            stat_copy(j, i).wait_send()
            final_copy(j, i).wait_send()

    for i in range(planes - 1):
        z_copy(i).wait_send()
    for d in range(1, x_count):
        x_copy(d).wait_send()
    for d in range(1, group):
        y_copy(d).wait_send()


def body(planes, ring, group, hq, hk, hv, og, ka, va, lists, counts):
    head_count = lists.shape[0]
    heads = head_count // planes
    width = heads * HEAD_WIDTH
    rank = ka.shape[-1]
    x_count = ring // group
    x_rows = width // x_count
    y_rows = x_rows // group
    y_pad = -(-y_rows // 8) * 8
    block = lax.axis_index("seq")
    own_lists = lax.dynamic_index_in_dim(lists, block, 1, keepdims=False)
    own_counts = lax.dynamic_index_in_dim(counts, block, 1, keepdims=False)
    used = jnp.arange(lists.shape[2])[None, :] < own_counts[:, None]
    holders = block + REACH - jnp.arange(WINDOW)
    live = jnp.any((own_lists[None] == holders[:, None, None]) & used[None], axis=2)
    bias = jnp.where(live, 0.0, -jnp.inf).astype(F32).reshape(WINDOW, planes, heads, 1)
    bias = jnp.broadcast_to(bias, (WINDOW, planes, heads, BLK))
    ka_wide = jnp.pad(ka[0], ((0, 0), (0, rank)))
    va_wide = jnp.pad(va[0], ((0, 0), (rank, 0)))
    tokens, columns = hq.shape[1:]
    sems = pltpu.SemaphoreType.DMA
    dk, dv, ad = pl.pallas_call(
        functools.partial(kernel, planes, ring, heads, group),
        out_shape=(
            jax.ShapeDtypeStruct((tokens, columns), BF16),
            jax.ShapeDtypeStruct((tokens, columns), BF16),
            jax.ShapeDtypeStruct((y_pad, 2 * rank), F32),
        ),
        in_specs=[pl.BlockSpec(memory_space=pltpu.VMEM)] * 7,
        out_specs=[pl.BlockSpec(memory_space=pltpu.VMEM)] * 3,
        scratch_shapes=[
            pltpu.VMEM((planes, WINDOW, BLK, width), BF16),
            pltpu.VMEM((planes, WINDOW, BLK, width), BF16),
            pltpu.VMEM((3, heads, WINDOW, BLK, BLK), F32),
            pltpu.VMEM((3, heads, WINDOW, BLK, BLK), F32),
            pltpu.VMEM((WINDOW, planes, 3, 8, BLK), F32),
            pltpu.VMEM((WINDOW, planes, 3, 8, BLK), F32),
            pltpu.VMEM((WINDOW, planes, 2, 8, BLK), F32),
            pltpu.VMEM((WINDOW, planes, 2, 8, BLK), F32),
            pltpu.VMEM((max(planes - 1, 1), width, 2 * rank), BF16),
            pltpu.VMEM((max(planes - 1, 1), width, 2 * rank), BF16),
            pltpu.VMEM((width, 2 * rank), F32),
            pltpu.VMEM((max(x_count - 1, 1), x_rows, 2 * rank), F32),
            pltpu.VMEM((x_rows, 2 * rank), F32),
            pltpu.VMEM((group, y_pad, 2 * rank), F32),
            pltpu.VMEM((group - 1, y_pad, 2 * rank), F32),
            sems((4, planes, 2)),
            sems((4, planes, 2)),
            sems((WINDOW, planes)),
            sems((WINDOW, planes)),
            sems((WINDOW, planes)),
            sems((WINDOW, planes)),
            sems((max(planes - 1, 1),)),
            sems((max(planes - 1, 1),)),
            sems((max(x_count - 1, 1),)),
            sems((max(x_count - 1, 1),)),
            sems((group - 1,)),
            sems((group - 1,)),
        ],
        compiler_params=pltpu.CompilerParams(
            collective_id=0, has_side_effects=True, vmem_limit_bytes=60 * 1024 * 1024
        ),
    )(hq[0], hk[0], hv[0], og[0], ka_wide, va_wide, bias)
    return dk[None], dv[None], ad[:y_rows, :rank], ad[:y_rows, rank:]


def solution(mesh, group=ROW_GROUP):
    split = P("dp", "seq", None)
    rows = P(("dp", "seq"), None)
    return jax.shard_map(
        functools.partial(body, mesh.shape["dp"], mesh.shape["seq"], group),
        mesh=mesh,
        in_specs=(split,) * 6 + (P(), P()),
        out_specs=(split, split, rows, rows),
        check_vma=False,
    )
```

time: 845 us -> 109 us (0.13)
  waiting for transfers between devices: 481 us -> 0 us
  other arithmetic: 108 us -> 0.13 us
  Pallas kernels: 0 us -> 99.9 us
  starting transfers between devices: 83.6 us -> 0 us
  local copies, waits for them, and re-layouts: 77 us -> 7.89 us
  matrix products: 50.3 us -> 0 us
  loops' own time: 24.6 us -> 0 us
  between operations: 14.7 us -> 0.72 us
    unnamed x2 -> x0, waiting for transfers between devices: 284 us -> none
    ppermute x10 -> x0, waiting for transfers between devices: 197 us -> none  [the longest x6 167 us: from_partner(): return lax.ppermute(block, axis, route)]
    pallas_call x0 -> x1, Pallas kernels: none -> 99.9 us  [body(): pl.pallas_call(functools.partial(kernel, planes, ring, heads, group), out...]
    ppermute x10 -> x0, starting transfers between devices: 83.6 us -> none  [the longest x6 64.5 us: from_partner(): return lax.ppermute(block, axis, route)]
    dot_general x56 -> x0, matrix products: 50.3 us -> none  [the longest x27 32.5 us: tile_scores(): jnp.einsum('qxd,qyd->qxy', query_tiles, key_block, preferred_element_type...]
    scatter-add x20 -> x0, other arithmetic: 45.2 us -> none  [the longest x9 24.3 us: gradient_pass(): value_acc.at[picked].add(value_add)]
    gather x45 -> x0, local copies, waits for them, and re-layouts: 30.9 us -> none  [the longest x27 16.1 us: tile_scores(): key_block = jnp.take(key_window, picked, axis=0)]
    another operation x9 -> x0, loops' own time: 24.6 us -> none  [the longest x3 8.39 us: head_gradients(): return lax.fori_loop(0, longest, gradient_pass, (empty, empty))]
  transfers between devices with their start and end apart: 11 -> 0, of which waited for: 11 -> 0; matrix products, arithmetic and copies ran while one was open for 1% -> 0% of each run, Pallas kernels for 0% -> 0%
where the time goes in v1:
time: 109 us
  Pallas kernels  99.9 us (92%)
  local copies, waits for them, and re-layouts  7.89 us (7%)
    pallas_call x1, Pallas kernels, body(): pl.pallas_call(functools.partial(kernel, planes, ring, heads, group), out...  99.9 us
    unnamed x17, local copies, waits for them, and re-layouts  4.83 us

profile of v1, /device:TPU:1, one launch (start us, length us, event | category | flops | bytes accessed | tf_op | source)
XLA Modules:
  0.0 108.7 jit_solution(7356955998106520750)
XLA Ops:
  0.6 0.0 copy-start
  0.6 0.0 copy-start.5
  0.7 0.0 copy-start.2
  0.7 0.7 copy-done.5
  1.4 0.2 dynamic-slice_reduce_fusion
  1.6 0.0 copy-done.2
  1.6 0.1 copy.20
  1.7 0.0 copy-start.3
  1.7 0.6 pad.8.ka
  2.3 0.1 copy-done.3
  2.4 0.1 copy.21
  2.5 0.7 pad.9.va
  3.2 0.0 copy-done
  3.2 0.1 constant_dynamic-slice_fusion
  3.3 0.1 copy.23
  3.4 0.1 and_reduce_fusion
  3.5 0.1 select_n.19
  3.6 0.8 broadcast_in_dim.26.bias
  4.4 99.9 %shard_map.111 = (bf16[128,3072]{1,0:T(8,128)(2,1)}, bf16[128,3072]{1,0:T(8,128)(2,1)}, f32[8,128]{1,0:T(8,128)}) custom-call(bf16[128,3072]{1,0:T(8,128)(2,1)} %bitcast.11, bf16[128,3072]{1,0:T(8,128)(2,1)} %bitcast.12, bf16[128,3072]{1,0:T(8,128)(2,1)} %bitcast.13, bf16[128,3072]{1,0:T(8,128)(2,1)} %bitcast.14, bf16[128,128]{1,0:T(8,128)(2,1)} %pad.8.ka, ...), custom_call_target="tpu_custom_call" | custom-call | tf_op jit(solution)/shard_map/pallas_call | solution.py:294
  104.3 0.0 copy-start.4
  104.3 0.7 copy-done.4
  105.0 0.7 fusion
  105.6 0.0 copy-start.1
  105.6 2.1 %copy.26 = bf16[1,128,3072]{2,1,0:T(8,128)(2,1)} copy(bf16[1,128,3072]{2,1,0:T(8,128)(2,1)} %bitcast.10) | data formatting | bytes 1572864
  107.8 0.0 copy-done.1
  107.8 0.9 copy.27
  (3 shorter events, 0.0 us)
Async XLA Ops:
  0.6 2.6 %copy-start = (s32[24,64,5]{1,0,2:T(8,128)S(1)}, s32[24,64,5]{1,0,2:T(8,128)}, u32[]{:S(2)}) copy-start(s32[24,64,5]{1,0,2:T(8,128)} %param.14) | copy-start | bytes 92164
  0.6 0.7 copy-start.5
  0.7 0.9 copy-start.2
  1.7 0.7 copy-start.3
  104.3 0.7 copy-start.4
  105.6 2.1 %copy-start.1 = (bf16[128,3072]{1,0:T(8,128)(2,1)S(1)}, bf16[128,3072]{1,0:T(8,128)(2,1)}, u32[]{:S(2)}) copy-start(bf16[128,3072]{1,0:T(8,128)(2,1)} %get-tuple-element.8) | copy-start | bytes 2359300

commit v2 on v1

--- a/solution.py
+++ b/solution.py
@@ -12,6 +12,9 @@
 REACH = 2
 WINDOW = 2 * REACH + 1
 ROW_GROUP = 16
+AHEAD = 2
+LAG_STATS = 2
+LAG_LAST = 4
 HUGE = 3.0e38
 MESH = pl.DeviceIdType.MESH
 F32 = jnp.float32
@@ -24,10 +27,10 @@
 
 def kernel(
     planes, ring, heads, group,
-    q, k, v, g, ka, va, bias,
-    dk, dv, ad,
-    hq, hg, es, ds, st, rs, fo, fr, zs, zr, own, xr, rows, ub, yr,
-    h_send, h_recv, s_send, s_recv, f_send, f_recv, z_send, z_recv, x_send, x_recv, y_send, y_recv,
+    q_hbm, k_hbm, v_hbm, g_hbm, ka, va, lists, counts,
+    dk_hbm, dv_hbm, ad,
+    q, k, v, g, dk, dv, wide, shut, hq, hg, es, ds, st, rs, fo, fr, zs, zr, own, xr, rows, ub, yr,
+    in_sem, out_sem, h_send, h_recv, s_send, s_recv, f_send, f_recv, z_send, z_recv, x_send, x_recv, y_send, y_recv,
 ):
     scaling = HEAD_WIDTH ** (-0.5)
     z = lax.axis_index("dp")
@@ -54,7 +57,9 @@
         return lax.rem(z + step, planes)
 
     def piece(step):
-        return lax.rem(z + 1 + step, planes)
+        odd = lax.rem(step, 2)
+        far = (step + odd) // 2
+        return lax.rem(z + planes // 2 + (2 * odd - 1) * far + planes, planes)
 
     def remote(src, dst, send, recv, device):
         return pltpu.make_async_remote_copy(
@@ -63,7 +68,7 @@
         )
 
     def halo(flow, i, a, landing=False):
-        source, store = (q, g)[a], (hq, hg)[a]
+        source, store = (q_hbm, g_hbm)[a], (hq, hg)[a]
         cols = pl.ds(pl.multiple_of(piece(i) * width, 128), width)
         if flow == 0:
             src, slot, to = source.at[:, cols], 0, peer(2)
@@ -86,7 +91,8 @@
         return remote(fo.at[j, i], fr.at[j, i], f_send.at[j, i], f_recv.at[j, i], (z, peer(2 - j)))
 
     def z_copy(i):
-        return remote(zs.at[i], zr.at[i], z_send.at[i], z_recv.at[i], (piece(i), pos))
+        onward = lax.rem(z + 1 - 2 * lax.rem(i, 2) + planes, planes)
+        return remote(zs.at[i], zr.at[i], z_send.at[i], z_recv.at[i], (onward, pos))
 
     def x_copy(d):
         there = lax.rem(x_at + d, x_count)
@@ -99,12 +105,34 @@
             ub.at[there], yr.at[d - 1], y_send.at[d - 1], y_recv.at[d - 1], (z, y_peer(d))
         )
 
+    def out_copy(i, a):
+        cols = pl.ds(pl.multiple_of(piece(i) * width, 128), width)
+        src, dst = ((dk, dk_hbm), (dv, dv_hbm))[a]
+        return pltpu.make_async_copy(src.at[:, cols], dst.at[:, cols], out_sem.at[i, a])
+
+    loads = [
+        pltpu.make_async_copy(src, dst, in_sem.at[n])
+        for n, (src, dst) in enumerate(((q_hbm, q), (k_hbm, k), (g_hbm, g), (v_hbm, v)))
+    ]
+    for load in loads:
+        load.start()
+    wide[...] = jnp.concatenate([ka[...], va[...]], axis=0).astype(F32).T.astype(BF16)
+    lane = lax.broadcasted_iota(jnp.int32, counts.shape, 1)
+    for j in range(WINDOW):
+        hits = [
+            (lists[n] == lane + (REACH - j)) & (counts[...] > n) & (lane == pos)
+            for n in range(lists.shape[0])
+        ]
+        found = sum(jnp.where(hit, 1.0, 0.0) for hit in hits)
+        column = jnp.sum(found, axis=1, keepdims=True)
+        shut[j] = jnp.broadcast_to(jnp.where(column > 0.5, 0.0, -jnp.inf), shut.shape[1:])
+
     barrier = pltpu.get_barrier_semaphore()
     greeted = 0
     for d in (-2, -1, 1, 2):
         pl.semaphore_signal(barrier, inc=1, device_id=(z, peer(d)), device_id_type=MESH)
         greeted += 1
-    for d in range(1, planes):
+    for d in (1, planes - 1):
         pl.semaphore_signal(barrier, inc=1, device_id=(z_peer(d), pos), device_id_type=MESH)
         greeted += 1
     for d in range(1, x_count):
@@ -115,11 +143,15 @@
         greeted += 1
     pl.semaphore_wait(barrier, greeted)
 
-    @pl.loop(0, planes)
-    def _(i):
-        for flow in (0, 1, 2):
-            for a in (0, 1):
+    def send_halo(i):
+        for a in (0, 1):
+            for flow in (0, 1, 2):
                 halo(flow, i, a).start()
+
+    for i in range(min(AHEAD, planes)):
+        send_halo(i)
+    for load in loads:
+        load.wait()
 
     def head_cols(i, h):
         return pl.ds(pl.multiple_of(piece(i) * width + h * HEAD_WIDTH, 128), HEAD_WIDTH)
@@ -130,7 +162,7 @@
         return store[i, j, :, h * HEAD_WIDTH : (h + 1) * HEAD_WIDTH]
 
     def tile_stats(i, h, j):
-        held = lax.rem(i, 3)
+        held = lax.rem(i, LAG_LAST + 1)
         scores = scaling * lax.dot_general(
             k[:, head_cols(i, h)], operand(q, hq, i, h, j), NT, preferred_element_type=F32
         )
@@ -145,17 +177,20 @@
         st[j, i, 1, h : h + 1, :] = jnp.sum(grown, axis=0, keepdims=True)
         st[j, i, 2, h : h + 1, :] = jnp.sum(grown * dprobs, axis=0, keepdims=True)
 
-    def first_pass(i):
-        for flow in (0, 1):
-            for a in (0, 1):
+    def arrive(i):
+        for a in (0, 1):
+            for flow in (0, 1):
                 halo(flow, i, a, True).wait_recv()
-        for a in (0, 1):
             halo(3, i, a).start()
+
+    def first_tiles(i):
         for a in (0, 1):
             halo(2, i, a, True).wait_recv()
         for h in range(heads):
             for j in (2, 0, 4, 3 - 2 * parity):
                 tile_stats(i, h, j)
+
+    def last_tiles(i):
         for a in (0, 1):
             halo(3, i, a, True).wait_recv()
         for h in range(heads):
@@ -166,11 +201,13 @@
     def combine(i):
         for j in OTHERS:
             stat_copy(j, i).wait_recv()
-        tops, totals, sums, shut = [], [], [], []
+        tops, totals, sums, dead = [], [], [], []
         for j in range(WINDOW):
             part = st if j == 2 else rs
-            closed = bias[j, piece(i)]
-            shut.append(closed)
+            closed = jnp.concatenate(
+                [shut[j, pl.ds(piece(i) * heads + h, 1), :] for h in range(heads)], axis=0
+            )
+            dead.append(closed < 0)
             tops.append(part[j, i, 0, 0:heads, :] + closed)
             totals.append(part[j, i, 1, 0:heads, :])
             sums.append(part[j, i, 2, 0:heads, :])
@@ -180,13 +217,13 @@
         delta = sum(w * t for w, t in zip(weights, sums)) / total
         level = top + jnp.log(total)
         for j in range(WINDOW):
-            fo[j, i, 0, 0:heads, :] = jnp.where(shut[j] < 0, HUGE, level)
+            fo[j, i, 0, 0:heads, :] = jnp.where(dead[j], HUGE, level)
             fo[j, i, 1, 0:heads, :] = delta
         for j in OTHERS:
             final_copy(j, i).start()
 
     def second_pass(i):
-        held = lax.rem(i, 3)
+        held = lax.rem(i, LAG_LAST + 1)
         for j in OTHERS:
             final_copy(j, i).wait_recv()
         for h in range(heads):
@@ -207,34 +244,52 @@
             value_out = value_sum.astype(BF16)
             dk[:, head_cols(i, h)] = key_out
             dv[:, head_cols(i, h)] = value_out
-            term = lax.dot_general(key_out, ka[...], TN, preferred_element_type=F32)
-            term += lax.dot_general(value_out, va[...], TN, preferred_element_type=F32)
+            key_term = lax.dot_general(key_out, wide[...], TN, preferred_element_type=F32)
+            value_term = lax.dot_general(value_out, wide[...], TN, preferred_element_type=F32)
+            side = lax.broadcasted_iota(jnp.int32, key_term.shape, 1)
+            term = jnp.where(side < ka.shape[0], key_term, value_term)
             own[h * HEAD_WIDTH : (h + 1) * HEAD_WIDTH, :] = term
+        for a in (0, 1):
+            out_copy(i, a).start()
+
+        @pl.when(i >= 2)
+        def _():
+            z_copy(i - 2).wait_recv()
+            own[...] += zr[i - 2].astype(F32)
 
         @pl.when(i < planes - 1)
         def _():
             zs[i] = own[...].astype(BF16)
             z_copy(i).start()
 
-    @pl.loop(0, planes + 2)
+    @pl.loop(0, planes + LAG_LAST)
     def _(t):
         @pl.when(t < planes)
         def _():
-            first_pass(t)
-
-        @pl.when((t >= 1) & (t < planes + 1))
-        def _():
-            combine(t - 1)
-
-        @pl.when(t >= 2)
-        def _():
-            second_pass(t - 2)
-
-    total = own[...]
-    for i in range(planes - 1):
-        z_copy(i).wait_recv()
-        total += zr[i].astype(F32)
-    own[...] = total
+            arrive(t)
+
+        @pl.when(t < planes - AHEAD)
+        def _():
+            send_halo(t + AHEAD)
+
+        @pl.when(t < planes)
+        def _():
+            first_tiles(t)
+
+        @pl.when((t >= LAG_STATS) & (t < planes + LAG_STATS))
+        def _():
+            combine(t - LAG_STATS)
+
+        @pl.when(t < planes)
+        def _():
+            last_tiles(t)
+
+        @pl.when(t >= LAG_LAST)
+        def _():
+            second_pass(t - LAG_LAST)
+
+    z_copy(planes - 2).wait_recv()
+    own[...] += zr[planes - 2].astype(F32)
     for d in range(1, x_count):
         x_copy(d).start()
     mine = own[pl.ds(pl.multiple_of(x_at * x_rows, 8), x_rows), :]
@@ -258,6 +313,8 @@
         for flow in range(4):
             for a in (0, 1):
                 halo(flow, i, a).wait_send()
+        for a in (0, 1):
+            out_copy(i, a).wait()
         for j in OTHERS:
             stat_copy(j, i).wait_send()
             final_copy(j, i).wait_send()
@@ -268,6 +325,25 @@
         x_copy(d).wait_send()
     for d in range(1, group):
         y_copy(d).wait_send()
+
+
+def finish(parts, part, dk, dv, ad, dk_out, dv_out, ka_grad, va_grad, hold, in_sem, out_sem):
+    ins, outs = [], []
+    for n in range(parts):
+        cols = pl.ds(n * part, part)
+        for a, (src, dst) in enumerate(((dk, dk_out), (dv, dv_out))):
+            ins.append(pltpu.make_async_copy(src.at[:, cols], hold.at[a, n], in_sem.at[a, n]))
+            outs.append(pltpu.make_async_copy(hold.at[a, n], dst.at[:, cols], out_sem.at[a, n]))
+    for load in ins:
+        load.start()
+    rank = ka_grad.shape[1]
+    ka_grad[...] = ad[0 : ka_grad.shape[0], 0:rank]
+    va_grad[...] = ad[0 : ka_grad.shape[0], rank:]
+    for load, store in zip(ins, outs):
+        load.wait()
+        store.start()
+    for store in outs:
+        store.wait()
 
 
 def body(planes, ring, group, hq, hk, hv, og, ka, va, lists, counts):
@@ -279,16 +355,6 @@
     x_rows = width // x_count
     y_rows = x_rows // group
     y_pad = -(-y_rows // 8) * 8
-    block = lax.axis_index("seq")
-    own_lists = lax.dynamic_index_in_dim(lists, block, 1, keepdims=False)
-    own_counts = lax.dynamic_index_in_dim(counts, block, 1, keepdims=False)
-    used = jnp.arange(lists.shape[2])[None, :] < own_counts[:, None]
-    holders = block + REACH - jnp.arange(WINDOW)
-    live = jnp.any((own_lists[None] == holders[:, None, None]) & used[None], axis=2)
-    bias = jnp.where(live, 0.0, -jnp.inf).astype(F32).reshape(WINDOW, planes, heads, 1)
-    bias = jnp.broadcast_to(bias, (WINDOW, planes, heads, BLK))
-    ka_wide = jnp.pad(ka[0], ((0, 0), (0, rank)))
-    va_wide = jnp.pad(va[0], ((0, 0), (rank, 0)))
     tokens, columns = hq.shape[1:]
     sems = pltpu.SemaphoreType.DMA
     dk, dv, ad = pl.pallas_call(
@@ -298,13 +364,18 @@
             jax.ShapeDtypeStruct((tokens, columns), BF16),
             jax.ShapeDtypeStruct((y_pad, 2 * rank), F32),
         ),
-        in_specs=[pl.BlockSpec(memory_space=pltpu.VMEM)] * 7,
-        out_specs=[pl.BlockSpec(memory_space=pltpu.VMEM)] * 3,
+        in_specs=[pl.BlockSpec(memory_space=pl.ANY)] * 4
+        + [pl.BlockSpec(memory_space=pltpu.VMEM)] * 4,
+        out_specs=[pl.BlockSpec(memory_space=pl.ANY)] * 2
+        + [pl.BlockSpec(memory_space=pltpu.VMEM)],
         scratch_shapes=[
+            *[pltpu.VMEM((tokens, columns), BF16)] * 6,
+            pltpu.VMEM((tokens, 2 * rank), BF16),
+            pltpu.VMEM((WINDOW, head_count, BLK), F32),
             pltpu.VMEM((planes, WINDOW, BLK, width), BF16),
             pltpu.VMEM((planes, WINDOW, BLK, width), BF16),
-            pltpu.VMEM((3, heads, WINDOW, BLK, BLK), F32),
-            pltpu.VMEM((3, heads, WINDOW, BLK, BLK), F32),
+            pltpu.VMEM((LAG_LAST + 1, heads, WINDOW, BLK, BLK), F32),
+            pltpu.VMEM((LAG_LAST + 1, heads, WINDOW, BLK, BLK), F32),
             pltpu.VMEM((WINDOW, planes, 3, 8, BLK), F32),
             pltpu.VMEM((WINDOW, planes, 3, 8, BLK), F32),
             pltpu.VMEM((WINDOW, planes, 2, 8, BLK), F32),
@@ -316,6 +387,8 @@
             pltpu.VMEM((x_rows, 2 * rank), F32),
             pltpu.VMEM((group, y_pad, 2 * rank), F32),
             pltpu.VMEM((group - 1, y_pad, 2 * rank), F32),
+            sems((4,)),
+            sems((planes, 2)),
             sems((4, planes, 2)),
             sems((4, planes, 2)),
             sems((WINDOW, planes)),
@@ -332,8 +405,28 @@
         compiler_params=pltpu.CompilerParams(
             collective_id=0, has_side_effects=True, vmem_limit_bytes=60 * 1024 * 1024
         ),
-    )(hq[0], hk[0], hv[0], og[0], ka_wide, va_wide, bias)
-    return dk[None], dv[None], ad[:y_rows, :rank], ad[:y_rows, rank:]
+    )(hq[0], hk[0], hv[0], og[0], ka[0].T, va[0].T, lists.transpose(2, 0, 1), counts)
+    parts = 4
+    part = columns // parts
+    dk, dv, ka_grad, va_grad = pl.pallas_call(
+        functools.partial(finish, parts, part),
+        out_shape=(
+            jax.ShapeDtypeStruct((tokens, columns), BF16),
+            jax.ShapeDtypeStruct((tokens, columns), BF16),
+            jax.ShapeDtypeStruct((y_rows, rank), F32),
+            jax.ShapeDtypeStruct((y_rows, rank), F32),
+        ),
+        in_specs=[pl.BlockSpec(memory_space=pl.ANY)] * 2
+        + [pl.BlockSpec(memory_space=pltpu.VMEM)],
+        out_specs=[pl.BlockSpec(memory_space=pl.ANY)] * 2
+        + [pl.BlockSpec(memory_space=pltpu.VMEM)] * 2,
+        scratch_shapes=[
+            pltpu.VMEM((2, parts, tokens, part), BF16),
+            sems((2, parts)),
+            sems((2, parts)),
+        ],
+    )(dk, dv, ad)
+    return dk[None], dv[None], ka_grad, va_grad
 
 
 def solution(mesh, group=ROW_GROUP):

time: 109 us -> 85.8 us (0.79)
  Pallas kernels: 99.9 us -> 84.9 us
  local copies, waits for them, and re-layouts: 7.89 us -> 0 us
    pallas_call x1, Pallas kernels: 99.9 us -> 81.3 us  [body(): pl.pallas_call(functools.partial(kernel, planes, ring, heads, group), out...]
    unnamed x17 -> x0, local copies, waits for them, and re-layouts: 4.83 us -> none
    pallas_call x0 -> x1, Pallas kernels: none -> 3.56 us  [body(): pl.pallas_call(functools.partial(finish, parts, part), out_shape=(jax.Sha...]
    pad x2 -> x0, local copies, waits for them, and re-layouts: 1.32 us -> none  [the longest x1 0.7 us: body(): va_wide = jnp.pad(va[0], ((0, 0), (rank, 0)))]
where the time goes in v2:
time: 85.8 us; the launch traced here: 85.6 us
  Pallas kernels  84.9 us (99%)
    pallas_call x1, Pallas kernels, body(): pl.pallas_call(functools.partial(kernel, planes, ring, heads, group), out...  81.3 us
    pallas_call x1, Pallas kernels, body(): pl.pallas_call(functools.partial(finish, parts, part), out_shape=(jax.Sha...  3.56 us

profile of v2, /device:TPU:1, one launch (start us, length us, event | category | flops | bytes accessed | tf_op | source)
XLA Modules:
  0.0 85.6 jit_solution(15948393198348933038)
XLA Ops:
  0.6 81.3 %shard_map.111 = (bf16[128,3072]{1,0:T(8,128)(2,1)}, bf16[128,3072]{1,0:T(8,128)(2,1)}, f32[8,128]{1,0:T(8,128)}) custom-call(bf16[128,3072]{1,0:T(8,128)(2,1)} %bitcast.13, bf16[128,3072]{1,0:T(8,128)(2,1)} %bitcast.14, bf16[128,3072]{1,0:T(8,128)(2,1)} %bitcast.15, bf16[128,3072]{1,0:T(8,128)(2,1)} %bitcast.16, bf16[64,128]{1,0:T(8,128)(2,1)} %bitcast.18, ...), custom_call_target="tpu_custom_call" | custom-call | tf_op jit(solution)/shard_map/pallas_call | solution.py:360
  82.0 3.6 %shard_map.112 = (bf16[128,3072]{1,0:T(8,128)(2,1)}, bf16[128,3072]{1,0:T(8,128)(2,1)}, f32[6,64]{1,0:T(8,128)}, f32[6,64]{1,0:T(8,128)}) custom-call(bf16[128,3072]{1,0:T(8,128)(2,1)} %get-tuple-element.11.dk, bf16[128,3072]{1,0:T(8,128)(2,1)} %get-tuple-element.12.dv, f32[8,128]{1,0:T(8,128)} %get-tuple-element.13.ad), custom_call_target="tpu_custom_call" | custom-call | tf_op jit(solution)/shard_map/pallas_call | solution.py:411

commit v3 on v2

--- a/solution.py
+++ b/solution.py
@@ -29,7 +29,7 @@
     planes, ring, heads, group,
     q_hbm, k_hbm, v_hbm, g_hbm, ka, va, lists, counts,
     dk_hbm, dv_hbm, ad,
-    q, k, v, g, dk, dv, wide, shut, hq, hg, es, ds, st, rs, fo, fr, zs, zr, own, xr, rows, ub, yr,
+    q, k, v, g, dk, dv, wide, shut, hq, hg, es, ds, st, rs, fo, fr, zs, zr, own, own16, xr, rows, ub, yr,
     in_sem, out_sem, h_send, h_recv, s_send, s_recv, f_send, f_recv, z_send, z_recv, x_send, x_recv, y_send, y_recv,
 ):
     scaling = HEAD_WIDTH ** (-0.5)
@@ -96,7 +96,7 @@
 
     def x_copy(d):
         there = lax.rem(x_at + d, x_count)
-        src = own.at[pl.ds(pl.multiple_of(there * x_rows, 8), x_rows)]
+        src = own16.at[pl.ds(pl.multiple_of(there * x_rows, 16), x_rows)]
         return remote(src, xr.at[d - 1], x_send.at[d - 1], x_recv.at[d - 1], (z, x_peer(d)))
 
     def y_copy(d):
@@ -173,9 +173,9 @@
         grown = jnp.exp(scores - top)
         es[held, h, j] = grown
         ds[held, h, j] = dprobs
-        st[j, i, 0, h : h + 1, :] = top
-        st[j, i, 1, h : h + 1, :] = jnp.sum(grown, axis=0, keepdims=True)
-        st[j, i, 2, h : h + 1, :] = jnp.sum(grown * dprobs, axis=0, keepdims=True)
+        st[j, i, h : h + 1, :] = top
+        st[j, i, heads + h : heads + h + 1, :] = jnp.sum(grown, axis=0, keepdims=True)
+        st[j, i, 2 * heads + h : 2 * heads + h + 1, :] = jnp.sum(grown * dprobs, axis=0, keepdims=True)
 
     def arrive(i):
         for a in (0, 1):
@@ -208,17 +208,17 @@
                 [shut[j, pl.ds(piece(i) * heads + h, 1), :] for h in range(heads)], axis=0
             )
             dead.append(closed < 0)
-            tops.append(part[j, i, 0, 0:heads, :] + closed)
-            totals.append(part[j, i, 1, 0:heads, :])
-            sums.append(part[j, i, 2, 0:heads, :])
+            tops.append(part[j, i, 0:heads, :] + closed)
+            totals.append(part[j, i, heads : 2 * heads, :])
+            sums.append(part[j, i, 2 * heads : 3 * heads, :])
         top = functools.reduce(jnp.maximum, tops)
         weights = [jnp.exp(t - top) for t in tops]
         total = sum(w * t for w, t in zip(weights, totals))
         delta = sum(w * t for w, t in zip(weights, sums)) / total
         level = top + jnp.log(total)
         for j in range(WINDOW):
-            fo[j, i, 0, 0:heads, :] = jnp.where(dead[j], HUGE, level)
-            fo[j, i, 1, 0:heads, :] = delta
+            fo[j, i, 0:heads, :] = jnp.where(dead[j], HUGE, level)
+            fo[j, i, heads : 2 * heads, :] = delta
         for j in OTHERS:
             final_copy(j, i).start()
 
@@ -231,9 +231,9 @@
             value_sum = jnp.zeros((BLK, HEAD_WIDTH), F32)
             for j in range(WINDOW):
                 final = fo if j == 2 else fr
-                factor = jnp.exp(st[j, i, 0, h : h + 1, :] - final[j, i, 0, h : h + 1, :])
+                factor = jnp.exp(st[j, i, h : h + 1, :] - final[j, i, h : h + 1, :])
                 probs = es[held, h, j] * factor
-                score_grad = (probs * (ds[held, h, j] - final[j, i, 1, h : h + 1, :])).astype(BF16)
+                score_grad = (probs * (ds[held, h, j] - final[j, i, heads + h : heads + h + 1, :])).astype(BF16)
                 value_sum += lax.dot_general(
                     probs.astype(BF16), operand(g, hg, i, h, j), NN, preferred_element_type=F32
                 )
@@ -280,22 +280,23 @@
         def _():
             combine(t - LAG_STATS)
 
+        @pl.when(t >= LAG_LAST)
+        def _():
+            second_pass(t - LAG_LAST)
+
         @pl.when(t < planes)
         def _():
             last_tiles(t)
-
-        @pl.when(t >= LAG_LAST)
-        def _():
-            second_pass(t - LAG_LAST)
 
     z_copy(planes - 2).wait_recv()
     own[...] += zr[planes - 2].astype(F32)
+    own16[...] = own[...].astype(BF16)
     for d in range(1, x_count):
         x_copy(d).start()
     mine = own[pl.ds(pl.multiple_of(x_at * x_rows, 8), x_rows), :]
     for d in range(1, x_count):
         x_copy(d).wait_recv()
-        mine += xr[d - 1]
+        mine += xr[d - 1].astype(F32)
     rows[...] = mine
     ub[...] = jnp.zeros_like(ub)
     for n in range(group):
@@ -376,14 +377,15 @@
             pltpu.VMEM((planes, WINDOW, BLK, width), BF16),
             pltpu.VMEM((LAG_LAST + 1, heads, WINDOW, BLK, BLK), F32),
             pltpu.VMEM((LAG_LAST + 1, heads, WINDOW, BLK, BLK), F32),
-            pltpu.VMEM((WINDOW, planes, 3, 8, BLK), F32),
-            pltpu.VMEM((WINDOW, planes, 3, 8, BLK), F32),
-            pltpu.VMEM((WINDOW, planes, 2, 8, BLK), F32),
-            pltpu.VMEM((WINDOW, planes, 2, 8, BLK), F32),
+            pltpu.VMEM((WINDOW, planes, 16, BLK), F32),
+            pltpu.VMEM((WINDOW, planes, 16, BLK), F32),
+            pltpu.VMEM((WINDOW, planes, 8, BLK), F32),
+            pltpu.VMEM((WINDOW, planes, 8, BLK), F32),
             pltpu.VMEM((max(planes - 1, 1), width, 2 * rank), BF16),
             pltpu.VMEM((max(planes - 1, 1), width, 2 * rank), BF16),
             pltpu.VMEM((width, 2 * rank), F32),
-            pltpu.VMEM((max(x_count - 1, 1), x_rows, 2 * rank), F32),
+            pltpu.VMEM((width, 2 * rank), BF16),
+            pltpu.VMEM((max(x_count - 1, 1), x_rows, 2 * rank), BF16),
             pltpu.VMEM((x_rows, 2 * rank), F32),
             pltpu.VMEM((group, y_pad, 2 * rank), F32),
             pltpu.VMEM((group - 1, y_pad, 2 * rank), F32),

time: 85.8 us -> 84.5 us (0.985)
  Pallas kernels: 84.9 us -> 83.6 us
    pallas_call x1, Pallas kernels: 81.3 us -> 80 us  [body(): pl.pallas_call(functools.partial(kernel, planes, ring, heads, group), out...]
where the time goes in v3:
time: 84.5 us; the launch traced here: 84.2 us
  Pallas kernels  83.6 us (99%)
    pallas_call x1, Pallas kernels, body(): pl.pallas_call(functools.partial(kernel, planes, ring, heads, group), out...  80 us
    pallas_call x1, Pallas kernels, body(): pl.pallas_call(functools.partial(finish, parts, part), out_shape=(jax.Sha...  3.56 us

profile of v3, /device:TPU:1, one launch (start us, length us, event | category | flops | bytes accessed | tf_op | source)
XLA Modules:
  0.0 84.2 jit_solution(10478532761293350805)
XLA Ops:
  0.6 80.0 %shard_map.111 = (bf16[128,3072]{1,0:T(8,128)(2,1)}, bf16[128,3072]{1,0:T(8,128)(2,1)}, f32[8,128]{1,0:T(8,128)}) custom-call(bf16[128,3072]{1,0:T(8,128)(2,1)} %bitcast.13, bf16[128,3072]{1,0:T(8,128)(2,1)} %bitcast.14, bf16[128,3072]{1,0:T(8,128)(2,1)} %bitcast.15, bf16[128,3072]{1,0:T(8,128)(2,1)} %bitcast.16, bf16[64,128]{1,0:T(8,128)(2,1)} %bitcast.18, ...), custom_call_target="tpu_custom_call" | custom-call | tf_op jit(solution)/shard_map/pallas_call | solution.py:361
  80.7 3.6 %shard_map.112 = (bf16[128,3072]{1,0:T(8,128)(2,1)}, bf16[128,3072]{1,0:T(8,128)(2,1)}, f32[6,64]{1,0:T(8,128)}, f32[6,64]{1,0:T(8,128)}) custom-call(bf16[128,3072]{1,0:T(8,128)(2,1)} %get-tuple-element.11.dk, bf16[128,3072]{1,0:T(8,128)(2,1)} %get-tuple-element.12.dv, f32[8,128]{1,0:T(8,128)} %get-tuple-element.13.ad), custom_call_target="tpu_custom_call" | custom-call | tf_op jit(solution)/shard_map/pallas_call | solution.py:413
